TPU v7x, 32 devices: a whole 2x2x4 slice. The times are simulated.
32 devices in a mesh: member: 8 (over z, x), tensor: 4 (over y, core).
Axes of the slice: x: 2, y: 2, z: 4, core: 2. Of those that a mesh axis runs over, the one named last changes fastest.
Arguments:
- tokens: bfloat16 [1024, 8192], P('member'), may hold values from -6 to 6
- out_grad: bfloat16 [1024, 8192], P('member'), may hold values from -6 to 6
- flip_bits: int32 [1024], P('member'), may hold values 0 or 1
- in_scale: float32 [8, 8192], P(None, 'member'), may hold values from 0.5 to 2
- out_scale: float32 [8, 8192], P(None, 'member'), may hold values from 0.5 to 2
- gate_scale: float32 [8, 14336], P('member', 'tensor'), may hold values from 0.5 to 2
- gate_flip: float32 [8, 14336], P('member', 'tensor'), may hold values from -2 to 2
- up_scale: float32 [8, 14336], P('member', 'tensor'), may hold values from 0.5 to 2
- up_flip: float32 [8, 14336], P('member', 'tensor'), may hold values from -2 to 2
- proj_gate: bfloat16 [1024, 14336], P('member', 'tensor'), may hold values from -6 to 6
- proj_up: bfloat16 [1024, 14336], P('member', 'tensor'), may hold values from -6 to 6
- w_gate: bfloat16 [8192, 14336], P('member', 'tensor'), may hold values from -0.0625 to 0.0625
- w_up: bfloat16 [8192, 14336], P('member', 'tensor'), may hold values from -0.0625 to 0.0625
- w_down: bfloat16 [14336, 8192], P('tensor', 'member'), may hold values from -0.046875 to 0.046875
Outputs:
- x_grad: bfloat16 [1024, 8192], P(('member', 'tensor'))
- w_gate_grad: bfloat16 [8192, 14336], P('member', 'tensor')
- w_up_grad: bfloat16 [8192, 14336], P('member', 'tensor')
- w_down_grad: bfloat16 [14336, 8192], P('tensor', 'member')
- in_scale_grad: float32 [8, 8192], P(None, 'member')
- out_scale_grad: float32 [8, 8192], P(None, 'member')
- gate_scale_grad: float32 [8, 14336], P('member', 'tensor')
- gate_flip_grad: float32 [8, 14336], P('member', 'tensor')
- up_scale_grad: float32 [8, 14336], P('member', 'tensor')
- up_flip_grad: float32 [8, 14336], P('member', 'tensor')
All inputs are finite; a program needn't handle non-finite values. No bound on the sum of `flip_bits` on one device may be relied on, other than what follows from the above.
Results may differ from a plain program's by a relative error of at most 0.024.
Values may be sent and summed in bfloat16 or wider, within the bound.
A program may use at most 128 MiB of HBM per device.

v0:
```python
import jax
import jax.numpy as jnp
from jax import lax
from jax.sharding import PartitionSpec as P


def scale_rows(block, table, rows):
    members, width = table.shape
    scaled = block.reshape(members, rows, width).astype(jnp.float32) * table[:, None, :]
    return scaled.reshape(members * rows, width)


def contract_rows(left, right):
    return lax.dot_general(
        left, right, (((0,), (0,)), ((), ())), preferred_element_type=jnp.float32
    )


def contract_cols(left, right):
    return lax.dot_general(
        left, right, (((1,), (1,)), ((), ())), preferred_element_type=jnp.float32
    )


def local(
    tokens,
    out_grad,
    flip_bits,
    in_scale,
    out_scale,
    gate_scale,
    gate_flip,
    up_scale,
    up_flip,
    proj_gate,
    proj_up,
    w_gate,
    w_up,
    w_down,
):
    rows = tokens.shape[0]
    members, width = in_scale.shape
    tensor_count = lax.axis_size("tensor")
    all_tokens, all_cotan = (
        lax.all_to_all(tokens, "member", split_axis=1, concat_axis=0, tiled=True),
        lax.all_to_all(out_grad, "member", split_axis=1, concat_axis=0, tiled=True),
    )
    in_rows = scale_rows(all_tokens, in_scale, rows).astype(jnp.bfloat16)
    grad_z = scale_rows(all_cotan, out_scale, rows).astype(jnp.bfloat16)
    grad_hidden = lax.psum_scatter(
        contract_cols(grad_z, w_down).astype(jnp.bfloat16),
        "member",
        scatter_dimension=0,
        tiled=True,
    ).astype(jnp.float32)
    sign = (2 * flip_bits - 1).astype(jnp.float32)[:, None]
    gate_factor = gate_scale + sign * gate_flip
    up_factor = up_scale + sign * up_flip
    pg_f = proj_gate.astype(jnp.float32)
    pu_f = proj_up.astype(jnp.float32)
    gate = pg_f * gate_factor
    up = pu_f * up_factor
    sig = jax.nn.sigmoid(gate)
    act = gate * sig
    hidden = (act * up).astype(jnp.bfloat16)
    grad_gate = grad_hidden * up * sig * (1.0 + gate * (1.0 - sig))
    grad_up = grad_hidden * act
    gate_scale_grad = jnp.sum(grad_gate * pg_f, axis=0, keepdims=True)
    gate_flip_grad = jnp.sum(sign * grad_gate * pg_f, axis=0, keepdims=True)
    up_scale_grad = jnp.sum(grad_up * pu_f, axis=0, keepdims=True)
    up_flip_grad = jnp.sum(sign * grad_up * pu_f, axis=0, keepdims=True)
    grad_pg = (grad_gate * gate_factor).astype(jnp.bfloat16)
    grad_pu = (grad_up * up_factor).astype(jnp.bfloat16)
    hid_piece = lax.all_gather(hidden, "member", axis=0, tiled=True)
    pg_piece = lax.all_gather(grad_pg, "member", axis=0, tiled=True)
    pu_piece = lax.all_gather(grad_pu, "member", axis=0, tiled=True)
    count = hid_piece.shape[0]
    groups = count // rows
    down_acc = contract_rows(hid_piece, grad_z)
    gate_acc = contract_rows(in_rows, pg_piece)
    up_acc = contract_rows(in_rows, pu_piece)
    grad_piece = contract_cols(pg_piece, w_gate) + contract_cols(pu_piece, w_up)
    grad_in = grad_piece
    in_terms = (
        (all_tokens.astype(jnp.float32) * grad_piece).reshape(groups, rows, width).sum(axis=1)
    )
    in_part = in_terms
    down_piece = jnp.dot(hid_piece, w_down, preferred_element_type=jnp.float32)
    out_terms = (
        (all_cotan.astype(jnp.float32) * down_piece).reshape(groups, rows, width).sum(axis=1)
    )
    out_part = out_terms
    down_acc, gate_acc, up_acc, grad_in, in_part, out_part = (
        down_acc,
        gate_acc,
        up_acc,
        grad_in,
        in_part,
        out_part,
    )
    in_scale_grad, out_scale_grad = (
        lax.psum(in_part.astype(jnp.bfloat16), "tensor").astype(jnp.float32),
        lax.psum(out_part.astype(jnp.bfloat16), "tensor").astype(jnp.float32),
    )
    scaled = grad_in.reshape(members, rows, width) * in_scale[:, None, :]
    summed = lax.psum_scatter(
        scaled.astype(jnp.bfloat16), "tensor", scatter_dimension=1, tiled=True
    ).astype(jnp.float32)
    returned = lax.all_to_all(
        summed.astype(jnp.bfloat16), "member", split_axis=0, concat_axis=2, tiled=True
    ).astype(summed.dtype)
    x_grad = returned.reshape(rows // tensor_count, members * width).astype(jnp.bfloat16)
    return (
        x_grad,
        gate_acc.astype(jnp.bfloat16),
        up_acc.astype(jnp.bfloat16),
        down_acc.astype(jnp.bfloat16),
        in_scale_grad,
        out_scale_grad,
        gate_scale_grad,
        gate_flip_grad,
        up_scale_grad,
        up_flip_grad,
    )


def solution(mesh):
    return jax.shard_map(
        local,
        mesh=mesh,
        in_specs=(
            P("member", None),
            P("member", None),
            P("member"),
            P(None, "member"),
            P(None, "member"),
            P("member", "tensor"),
            P("member", "tensor"),
            P("member", "tensor"),
            P("member", "tensor"),
            P("member", "tensor"),
            P("member", "tensor"),
            P("member", "tensor"),
            P("member", "tensor"),
            P("tensor", "member"),
        ),
        out_specs=(
            P(("member", "tensor"), None),
            P("member", "tensor"),
            P("member", "tensor"),
            P("tensor", "member"),
            P(None, "member"),
            P(None, "member"),
            P("member", "tensor"),
            P("member", "tensor"),
            P("member", "tensor"),
            P("member", "tensor"),
        ),
        check_vma=False,
    )
```

profile of v0, /device:TPU:0, one launch (start us, length us, event | category | flops | bytes accessed | tf_op | source)
XLA Modules:
  0.0 658.5 jit_solution(12860040867740411838)
XLA Ops:
  7.2 1.8 copy.34
  9.0 55.6 %all_to_all.44 = bf16[128,8,1024]{2,0,1:T(8,128)(2,1)S(1)} all-to-all(bf16[128,8,1024]{2,0,1:T(8,128)(2,1)S(1)} %bitcast.57), channel_id=1, replica_groups=mesh['member'=8,'tensor'=4] {'member'}, dimensions={1} | all-to-all | bytes 4194304 | tf_op jit(solution)/shard_map/all_to_all | solution.py:46
  65.2 1.4 copy-done.1
  66.5 9.9 %convolution_convert_fusion.3 = bf16[1024,3584]{1,0:T(8,128)(2,1)} fusion(bf16[1024,1024]{1,0:T(8,128)(2,1)S(1)} %fusion, bf16[3584,1024]{1,0:T(8,128)(2,1)S(1)} %copy-done.10), kind=kOutput, calls=%fused_computation.3 | convolution fusion | flops 7519862784 | bytes 16777216 | tf_op jit(solution)/shard_map/dot_general | solution.py:20
  77.3 131.2 %reduce-scatter.3.cloned.1.call-done = bf16[128,3584]{1,0:T(8,128)(2,1)} async-done(((bf16[1024,3584]{1,0:T(8,128)(2,1)}), bf16[128,3584]{1,0:T(8,128)(2,1)}) %reduce-scatter.3.cloned.1.call-update) | async-done | bytes 917520 | tf_op jit(solution)/shard_map/reduce_scatter | solution.py:50
  208.5 4.4 fusion.5
  212.9 1.2 multiply_convert_fusion.3
  215.5 1.8 copy.33
  217.3 81.4 %all_to_all.45 = bf16[128,8,1024]{2,0,1:T(8,128)(2,1)S(1)} all-to-all(bf16[128,8,1024]{2,0,1:T(8,128)(2,1)S(1)} %bitcast.58), channel_id=1, replica_groups=mesh['member'=8,'tensor'=4] {'member'}, dimensions={1} | all-to-all | bytes 4194304 | tf_op jit(solution)/shard_map/all_to_all | solution.py:45
  298.8 2.1 fusion.1
  303.3 57.7 %all-gather.4.cloned.1.call-done = bf16[1024,3584]{1,0:T(8,128)(2,1)} async-done(((bf16[128,3584]{1,0:T(8,128)(2,1)}), bf16[1024,3584]{1,0:T(8,128)(2,1)}) %all-gather.4.cloned.1.call-update) | async-done | bytes 7340048 | tf_op jit(solution)/shard_map/all_gather | solution.py:75
  361.0 13.5 %fusion.10 = f32[1024,1024]{1,0:T(8,128)} fusion(bf16[1024,3584]{1,0:T(8,128)(2,1)} %all-gather.4.cloned.1.call-done, bf16[1024,3584]{1,0:T(8,128)(2,1)} %param.25), kind=kOutput, calls=%fused_computation.38 | convolution fusion | flops 7516192768 | bytes 18874368 | tf_op jit(solution)/shard_map/dot_general | solution.py:20
  374.4 98.8 %all-gather.6.cloned.1.call-done = bf16[1024,3584]{1,0:T(8,128)(2,1)} async-done(((bf16[128,3584]{1,0:T(8,128)(2,1)}), bf16[1024,3584]{1,0:T(8,128)(2,1)}) %all-gather.6.cloned.1.call-update) | async-done | bytes 7340048 | tf_op jit(solution)/shard_map/all_gather | solution.py:76
  473.2 13.5 %bitcast_reduce_fusion.1 = (bf16[8,1024]{1,0:T(8,128)(2,1)S(1)}, f32[1024,1024]{1,0:T(8,128)S(1)}) fusion(bf16[128,8,1024]{2,0,1:T(8,128)(2,1)} %copy-done, f32[1024,1024]{1,0:T(8,128)} %fusion.10, bf16[1024,3584]{1,0:T(8,128)(2,1)} %all-gather.6.cloned.1.call-done, bf16[1024,3584]{1,0:T(8,128)(2,1)} %param.26), kind=kOutput, calls=%fused_computation.8 | convolution fusion | flops 7520378880 | bytes 25182208 | tf_op jit(solution)/shard_map/dot_general | solution.py:20
  486.7 1.9 multiply_convert_fusion
  488.7 96.8 %all-gather.8.cloned.1.call-done = bf16[1024,3584]{1,0:T(8,128)(2,1)} async-done(((bf16[128,3584]{1,0:T(8,128)(2,1)}), bf16[1024,3584]{1,0:T(8,128)(2,1)}) %all-gather.8.cloned.1.call-update) | async-done | bytes 7340048 | tf_op jit(solution)/shard_map/all_gather | solution.py:74
  585.5 12.2 %bitcast_reduce_fusion = bf16[8,1024]{1,0:T(8,128)(2,1)S(1)} fusion(bf16[128,8,1024]{2,0,1:T(8,128)(2,1)S(1)} %all_to_all.44, bf16[1024,3584]{1,0:T(8,128)(2,1)} %all-gather.8.cloned.1.call-done, bf16[3584,1024]{1,0:T(8,128)(2,1)} %param.27), kind=kOutput, calls=%fused_computation.4 | convolution fusion | flops 7519330304 | bytes 16793600 | tf_op jit(solution)/shard_map/dot_general | solution.py:88
  597.7 11.4 %all-reduce = (bf16[8,1024]{1,0:T(8,128)(2,1)S(1)}, bf16[8,1024]{1,0:T(8,128)(2,1)S(1)}) all-reduce(bf16[8,1024]{1,0:T(8,128)(2,1)S(1)} %get-tuple-element.21, bf16[8,1024]{1,0:T(8,128)(2,1)S(1)} %bitcast_reduce_fusion), channel_id=1, replica_groups=mesh['member'=8,'tensor'=4] {'tensor'}, use_global_device_ids=true, to_apply=%region_3.0 | all-reduce | flops 16384 | bytes 65536 | tf_op jit(solution)/shard_map/psum | solution.py:102
  610.4 12.8 %convolution_convert_fusion.2 = bf16[1024,3584]{1,0:T(8,128)(2,1)} fusion(bf16[1024,1024]{1,0:T(8,128)(2,1)} %fusion.1, bf16[1024,3584]{1,0:T(8,128)(2,1)} %all-gather.4.cloned.1.call-done), kind=kOutput, calls=%fused_computation.2 | convolution fusion | flops 7519862784 | bytes 16777216 | tf_op jit(solution)/shard_map/dot_general | solution.py:14
  623.2 10.0 %convolution_convert_fusion = bf16[3584,1024]{1,0:T(8,128)(2,1)} fusion(bf16[1024,3584]{1,0:T(8,128)(2,1)S(1)} %copy-done.11, bf16[1024,1024]{1,0:T(8,128)(2,1)S(1)} %copy-done.2), kind=kOutput, calls=%fused_computation | convolution fusion | flops 7519862784 | bytes 16777216 | tf_op jit(solution)/shard_map/dot_general | solution.py:14
  633.2 3.8 all-to-all-start.1
  637.0 12.7 %convolution_convert_fusion.1 = bf16[1024,3584]{1,0:T(8,128)(2,1)} fusion(bf16[1024,1024]{1,0:T(8,128)(2,1)} %fusion.1, bf16[1024,3584]{1,0:T(8,128)(2,1)} %all-gather.6.cloned.1.call-done), kind=kOutput, calls=%fused_computation.1 | convolution fusion | flops 7519862784 | bytes 16777216 | tf_op jit(solution)/shard_map/dot_general | solution.py:14
  649.6 1.5 all-to-all-done.1
  651.2 0.8 copy.29
  (48 shorter events, 6.5 us)
Async XLA Ops:
  7.2 201.3 %reduce-scatter.3.cloned.1.call-start = ((), (), s32[]{:S(2)}) async-start(), calls=%async_computation.5 | async-start | bytes 8257536 | tf_op jit(solution)/shard_map/reduce_scatter | solution.py:50
  9.0 55.6 %copy-start.5 = (f32[8,1024]{1,0:T(8,128)S(1)}, f32[8,1024]{1,0:T(8,128)}, u32[]{:S(2)}) copy-start(f32[8,1024]{1,0:T(8,128)} %param.18) | copy-start | bytes 98308
  9.0 57.5 %copy-start.10 = (bf16[3584,1024]{1,0:T(8,128)(2,1)S(1)}, bf16[3584,1024]{1,0:T(8,128)(2,1)}, u32[]{:S(2)}) copy-start(bf16[3584,1024]{1,0:T(8,128)(2,1)} %param.27) | copy-start | bytes 22020100
  65.1 1.4 copy-start.1
  76.4 0.7 copy-start.6
  76.4 0.8 copy-start.7
  76.4 0.8 copy-start.8
  76.4 0.9 copy-start.9
  76.4 0.9 copy-start.12
  76.4 132.1 %copy-start.3 = (bf16[128,3584]{1,0:T(8,128)(2,1)S(1)}, bf16[128,3584]{1,0:T(8,128)(2,1)}, u32[]{:S(2)}) copy-start(bf16[128,3584]{1,0:T(8,128)(2,1)} %param.24) | copy-start | bytes 2752516
  76.4 284.5 %all-gather.4.cloned.1.call-start = ((), (), s32[]{:S(2)}) async-start(), calls=%async_computation.6 | async-start | bytes 8257536 | tf_op jit(solution)/shard_map/all_gather | solution.py:75
  214.2 259.1 %all-gather.6.cloned.1.call-start = ((), (), s32[]{:S(2)}) async-start(), calls=%async_computation.7 | async-start | bytes 8257536 | tf_op jit(solution)/shard_map/all_gather | solution.py:76
  214.9 370.6 %all-gather.8.cloned.1.call-start = ((), (), s32[]{:S(2)}) async-start(), calls=%async_computation.9 | async-start | bytes 8257536 | tf_op jit(solution)/shard_map/all_gather | solution.py:74
  215.5 417.7 %reduce-scatter.5.cloned.1.call-start = ((), (), s32[]{:S(2)}) async-start(), calls=%async_computation.8 | async-start | bytes 2621440 | tf_op jit(solution)/shard_map/reduce_scatter | solution.py:106
  217.3 81.4 %copy-start.4 = (f32[8,1024]{1,0:T(8,128)S(1)}, f32[8,1024]{1,0:T(8,128)}, u32[]{:S(2)}) copy-start(f32[8,1024]{1,0:T(8,128)} %param.17) | copy-start | bytes 98308
  298.8 2.1 copy-start
  610.4 12.8 %copy-start.2 = (bf16[1024,1024]{1,0:T(8,128)(2,1)S(1)}, bf16[1024,1024]{1,0:T(8,128)(2,1)}, u32[]{:S(2)}) copy-start(bf16[1024,1024]{1,0:T(8,128)(2,1)} %copy-done.1) | copy-start | bytes 6291460
  610.4 12.8 %copy-start.11 = (bf16[1024,3584]{1,0:T(8,128)(2,1)S(1)}, bf16[1024,3584]{1,0:T(8,128)(2,1)}, u32[]{:S(2)}) copy-start(bf16[1024,3584]{1,0:T(8,128)(2,1)} %all-gather.8.cloned.1.call-done) | copy-start | bytes 22020100
  633.2 18.0 %all-to-all-start.1 = ((bf16[8,32,1024]{2,1,0:T(8,128)(2,1)}), bf16[8,32,1024]{2,1,0:T(8,128)(2,1)S(1)}, u32[]{:S(2)}, u32[]{:S(2)}) async-start(bf16[8,32,1024]{2,1,0:T(8,128)(2,1)} %reduce-scatter.5.cloned.1.call-done), calls=%async_computation.3 | async-start | bytes 1048576 | tf_op jit(solution)/shard_map/all_to_all | solution.py:109
Sparse Core Ops, SparseCore 0:
  76.5 131.8 reduce-scatter.2
  214.3 146.6 all-gather.3
  363.2 110.0 all-gather.5
  475.8 109.6 all-gather.7
  588.5 29.6 reduce-scatter.4
where the time goes:
time: 659 us
  waiting for transfers between devices  387 us (59%)
  blocking collectives  148 us (22%)
  matrix products  84.5 us (13%)
  between operations  14 us (2%)
  other arithmetic  11.6 us (2%)
  local copies, waits for them, and re-layouts  8.85 us (1%)
    reduce_scatter x1, waiting for transfers between devices, local(): lax.psum_scatter(contract_cols(grad_z, w_down).astype(jnp.bfloat16), 'mem...  131 us
    all_gather x1, waiting for transfers between devices, local(): pu_piece = lax.all_gather(grad_pu, 'member', axis=0, tiled=True)  98.8 us
    all_gather x1, waiting for transfers between devices, local(): hid_piece = lax.all_gather(hidden, 'member', axis=0, tiled=True)  96.8 us
    all_to_all x1, blocking collectives, local(): lax.all_to_all(tokens, 'member', split_axis=1, concat_axis=0, tiled=True)  81.4 us
    all_gather x1, waiting for transfers between devices, local(): pg_piece = lax.all_gather(grad_pg, 'member', axis=0, tiled=True)  57.7 us
    all_to_all x1, blocking collectives, local(): lax.all_to_all(out_grad, 'member', split_axis=1, concat_axis=0, tiled=True)  55.6 us
    dot_general x3, matrix products, contract_cols(): lax.dot_general(left, right, (((1,), (1,)), ((), ())), preferred_element_...  36.8 us
    dot_general x3, matrix products, contract_rows(): lax.dot_general(left, right, (((0,), (0,)), ((), ())), preferred_element_...  35.5 us
  transfers between devices with their start and end apart: 6, of which 5 were waited for; matrix products, arithmetic and copies ran while one was open for 13% of the time, Pallas kernels for 0%

commit v1 on v0

--- a/solution.py
+++ b/solution.py
@@ -2,6 +2,12 @@
 import jax.numpy as jnp
 from jax import lax
 from jax.sharding import PartitionSpec as P
+
+
+def joined_along(tiles, dim):
+    tiles = jnp.moveaxis(tiles, 0, dim)
+    dims = tiles.shape
+    return tiles.reshape(*dims[:dim], dims[dim] * dims[dim + 1], *dims[dim + 2 :])
 
 
 def scale_rows(block, table, rows):
@@ -73,7 +79,14 @@
     grad_pu = (grad_up * up_factor).astype(jnp.bfloat16)
     hid_piece = lax.all_gather(hidden, "member", axis=0, tiled=True)
     pg_piece = lax.all_gather(grad_pg, "member", axis=0, tiled=True)
-    pu_piece = lax.all_gather(grad_pu, "member", axis=0, tiled=True)
+    peers = lax.axis_size("member")
+    right_2 = [(i, (i + 1) % peers) for i in range(peers)]
+    blocks = [grad_pu]
+    while len(blocks) < peers:
+        blocks.append(lax.ppermute(blocks[-1], "member", right_2))
+    index = lax.axis_index("member")
+    blocks = jnp.stack(blocks)[(index - jnp.arange(peers)) % peers]
+    pu_piece = joined_along(blocks, 0)
     count = hid_piece.shape[0]
     groups = count // rows
     down_acc = contract_rows(hid_piece, grad_z)

time: 659 us -> 673 us (1.021)
  blocking collectives: 148 us -> 67 us
  starting transfers between devices: 3.95 us -> 67.2 us
  local copies, waits for them, and re-layouts: 8.85 us -> 30.6 us
  other arithmetic: 11.6 us -> 19.2 us
    ppermute x0 -> x7, waiting for transfers between devices: none -> 119 us  [local(): blocks.append(lax.ppermute(blocks[-1], 'member', right_2))]
    all_gather x1 -> x0, waiting for transfers between devices: 98.8 us -> none  [local(): pu_piece = lax.all_gather(grad_pu, 'member', axis=0, tiled=True)]
    all_to_all x1 -> x0, blocking collectives: 81.4 us -> none  [local(): lax.all_to_all(tokens, 'member', split_axis=1, concat_axis=0, tiled=True)]
    all_to_all x0 -> x1, waiting for transfers between devices: none -> 71.7 us  [local(): lax.all_to_all(tokens, 'member', split_axis=1, concat_axis=0, tiled=True)]
    ppermute x0 -> x7, starting transfers between devices: none -> 59.8 us  [local(): blocks.append(lax.ppermute(blocks[-1], 'member', right_2))]
    all_gather x1, waiting for transfers between devices: 57.7 us -> 0.01 us  [local(): pg_piece = lax.all_gather(grad_pg, 'member', axis=0, tiled=True)]
    all_gather x1, waiting for transfers between devices: 96.8 us -> 64.2 us  [local(): hid_piece = lax.all_gather(hidden, 'member', axis=0, tiled=True)]
    gather x0 -> x1, local copies, waits for them, and re-layouts: none -> 7.15 us  [local(): blocks = jnp.stack(blocks)[(index - jnp.arange(peers)) % peers]]
  transfers between devices with their start and end apart: 6 -> 13, of which waited for: 5 -> 10; matrix products, arithmetic and copies ran while one was open for 13% -> 17% of each run, Pallas kernels for 0% -> 0%
where the time goes in v1:
time: 673 us; the launch traced here: 672 us
  waiting for transfers between devices  388 us (58%)
  matrix products  86 us (13%)
  starting transfers between devices  67.2 us (10%)
  blocking collectives  67 us (10%)
  local copies, waits for them, and re-layouts  30.6 us (5%)
  other arithmetic  19.2 us (3%)
  between operations  14 us (2%)
    reduce_scatter x1, waiting for transfers between devices, local(): lax.psum_scatter(contract_cols(grad_z, w_down).astype(jnp.bfloat16), 'mem...  131 us
    ppermute x7, waiting for transfers between devices, local(): blocks.append(lax.ppermute(blocks[-1], 'member', right_2))  119 us
    all_to_all x1, waiting for transfers between devices, local(): lax.all_to_all(tokens, 'member', split_axis=1, concat_axis=0, tiled=True)  71.7 us
    all_gather x1, waiting for transfers between devices, local(): hid_piece = lax.all_gather(hidden, 'member', axis=0, tiled=True)  64.2 us
    ppermute x7, starting transfers between devices, local(): blocks.append(lax.ppermute(blocks[-1], 'member', right_2))  59.8 us
    all_to_all x1, blocking collectives, local(): lax.all_to_all(out_grad, 'member', split_axis=1, concat_axis=0, tiled=True)  55.6 us
    dot_general x3, matrix products, contract_rows(): lax.dot_general(left, right, (((0,), (0,)), ((), ())), preferred_element_...  38.8 us
    dot_general x3, matrix products, contract_cols(): lax.dot_general(left, right, (((1,), (1,)), ((), ())), preferred_element_...  34.8 us
  transfers between devices with their start and end apart: 13, of which 10 were waited for; matrix products, arithmetic and copies ran while one was open for 17% of the time, Pallas kernels for 0%

profile of v1, /device:TPU:0, one launch (start us, length us, event | category | flops | bytes accessed | tf_op | source)
XLA Modules:
  0.0 672.3 jit_solution(3255910337599807434)
XLA Ops:
  9.0 55.6 %all_to_all.44 = bf16[128,8,1024]{2,0,1:T(8,128)(2,1)S(1)} all-to-all(bf16[128,8,1024]{2,0,1:T(8,128)(2,1)S(1)} %bitcast.78), channel_id=1, replica_groups=mesh['member'=8,'tensor'=4] {'member'}, dimensions={1} | all-to-all | bytes 4194304 | tf_op jit(solution)/shard_map/all_to_all | solution.py:52
  66.6 9.9 %convolution_convert_fusion.2 = bf16[1024,3584]{1,0:T(8,128)(2,1)} fusion(bf16[1024,1024]{1,0:T(8,128)(2,1)S(1)} %fusion.1, bf16[3584,1024]{1,0:T(8,128)(2,1)S(1)} %copy-done.12), kind=kOutput, calls=%fused_computation.4 | convolution fusion | flops 7519862784 | bytes 16777216 | tf_op jit(solution)/shard_map/dot_general | solution.py:26
  77.4 131.2 %reduce-scatter.3.cloned.1.call-done = bf16[128,3584]{1,0:T(8,128)(2,1)} async-done(((bf16[1024,3584]{1,0:T(8,128)(2,1)}), bf16[128,3584]{1,0:T(8,128)(2,1)}) %reduce-scatter.3.cloned.1.call-update) | async-done | bytes 917520 | tf_op jit(solution)/shard_map/reduce_scatter | solution.py:56
  208.6 4.2 fusion.9
  228.0 71.7 %all-to-all-done.2 = bf16[128,8,1024]{0,2,1:T(8,128)(2,1)S(1)} async-done(((bf16[128,8,1024]{0,2,1:T(8,128)(2,1)}), bf16[128,8,1024]{0,2,1:T(8,128)(2,1)S(1)}, u32[]{:S(2)}, u32[]{:S(2)}) %all-to-all-start.2) | async-done | bytes 2097184 | tf_op jit(solution)/shard_map/all_to_all | solution.py:51
  302.0 5.4 copy.27
  307.4 4.1 fusion.2
  314.0 39.6 %collective-permute-start.1 = (bf16[128,3584]{1,0:T(8,128)(2,1)S(1)}, bf16[128,3584]{1,0:T(8,128)(2,1)S(1)}, u32[]{:S(2)}, u32[]{:S(2)}) collective-permute-start(bf16[128,3584]{1,0:T(8,128)(2,1)S(1)} %collective-permute-done), channel_id=1, source_target_pairs={{0,4},{4,8},{8,12},{12,16},{16,20},{20,24},{24,28},{28,0},{1,5},{5... | collective-permute-start | bytes 2752520 | tf_op jit(solution)/shard_map/ppermute | solution.py:86
  354.5 21.1 %collective-permute-done.1 = bf16[128,3584]{1,0:T(8,128)(2,1)S(1)} collective-permute-done((bf16[128,3584]{1,0:T(8,128)(2,1)S(1)}, bf16[128,3584]{1,0:T(8,128)(2,1)S(1)}, u32[]{:S(2)}, u32[]{:S(2)}) %collective-permute-start.1) | collective-permute-done | bytes 917536 | tf_op jit(solution)/shard_map/ppermute | solution.py:86
  375.6 16.1 %collective-permute-start.2 = (bf16[128,3584]{1,0:T(8,128)(2,1)S(1)}, bf16[128,3584]{1,0:T(8,128)(2,1)S(1)}, u32[]{:S(2)}, u32[]{:S(2)}) collective-permute-start(bf16[128,3584]{1,0:T(8,128)(2,1)S(1)} %collective-permute-done.1), channel_id=1, source_target_pairs={{0,4},{4,8},{8,12},{12,16},{16,20},{20,24},{24,28},{28,0},{1,5},{5... | collective-permute-start | bytes 2752520 | tf_op jit(solution)/shard_map/ppermute | solution.py:86
  392.7 24.6 %collective-permute-done.2 = bf16[128,3584]{1,0:T(8,128)(2,1)S(1)} collective-permute-done((bf16[128,3584]{1,0:T(8,128)(2,1)S(1)}, bf16[128,3584]{1,0:T(8,128)(2,1)S(1)}, u32[]{:S(2)}, u32[]{:S(2)}) %collective-permute-start.2) | collective-permute-done | bytes 917536 | tf_op jit(solution)/shard_map/ppermute | solution.py:86
  419.7 18.0 %collective-permute-done.3 = bf16[128,3584]{1,0:T(8,128)(2,1)S(1)} collective-permute-done((bf16[128,3584]{1,0:T(8,128)(2,1)S(1)}, bf16[128,3584]{1,0:T(8,128)(2,1)S(1)}, u32[]{:S(2)}, u32[]{:S(2)}) %collective-permute-start.3) | collective-permute-done | bytes 917536 | tf_op jit(solution)/shard_map/ppermute | solution.py:86
  438.7 19.5 %collective-permute-done.4 = bf16[128,3584]{1,0:T(8,128)(2,1)S(1)} collective-permute-done((bf16[128,3584]{1,0:T(8,128)(2,1)S(1)}, bf16[128,3584]{1,0:T(8,128)(2,1)S(1)}, u32[]{:S(2)}, u32[]{:S(2)}) %collective-permute-start.4) | collective-permute-done | bytes 917536 | tf_op jit(solution)/shard_map/ppermute | solution.py:86
  459.2 19.5 %collective-permute-done.5 = bf16[128,3584]{1,0:T(8,128)(2,1)S(1)} collective-permute-done((bf16[128,3584]{1,0:T(8,128)(2,1)S(1)}, bf16[128,3584]{1,0:T(8,128)(2,1)S(1)}, u32[]{:S(2)}, u32[]{:S(2)}) %collective-permute-start.5) | collective-permute-done | bytes 917536 | tf_op jit(solution)/shard_map/ppermute | solution.py:86
  480.5 16.3 %collective-permute-done.6 = bf16[128,3584]{1,0:T(8,128)(2,1)S(1)} collective-permute-done((bf16[128,3584]{1,0:T(8,128)(2,1)S(1)}, bf16[128,3584]{1,0:T(8,128)(2,1)S(1)}, u32[]{:S(2)}, u32[]{:S(2)}) %collective-permute-start.6) | collective-permute-done | bytes 917536 | tf_op jit(solution)/shard_map/ppermute | solution.py:86
  497.7 7.1 %gather_fusion = bf16[8,128,3584]{2,1,0:T(8,128)(2,1)} fusion(bf16[8,128,3584]{2,1,0:T(8,128)(2,1)} %bitcast_dynamic-update-slice_fusion, s32[1024]{0:T(1024)S(1)} %pad_clamp_fusion), kind=kCustom, calls=%fused_computation | custom fusion | bytes 14680096 | tf_op jit(solution)/shard_map/gather | solution.py:88
  504.9 14.2 %fusion.16 = f32[1024,1024]{1,0:T(8,128)} fusion(bf16[1024,3584]{1,0:T(8,128)(2,1)} %all-gather.3.cloned.1.call-done, bf16[1024,3584]{1,0:T(8,128)(2,1)} %param.25), kind=kOutput, calls=%fused_computation.58 | convolution fusion | flops 7516192768 | bytes 18874368 | tf_op jit(solution)/shard_map/dot_general | solution.py:26
  519.1 10.8 %bitcast_reduce_fusion.1 = (bf16[8,1024]{1,0:T(8,128)(2,1)S(1)}, f32[1024,1024]{1,0:T(8,128)S(1)}) fusion(f32[8,128,1024]{2,1,0:T(8,128)S(1)} %copy-done, f32[1024,1024]{1,0:T(8,128)} %fusion.16, bf16[1024,3584]{1,0:T(8,128)(2,1)S(1)} %bitcast.79, bf16[1024,3584]{1,0:T(8,128)(2,1)} %param.26), kind=kOutput, calls=%fused_computation.12 | convolution fusion | flops 7519330304 | bytes 27279360 | tf_op jit(solution)/shard_map/dot_general | solution.py:26
  531.8 13.0 %bitcast_convert_fusion = bf16[1024,3584]{1,0:T(8,128)(2,1)} fusion(bf16[8,128,3584]{2,1,0:T(8,128)(2,1)} %gather_fusion, bf16[128,8,1024]{0,2,1:T(8,128)(2,1)S(1)} %all-to-all-done.2, f32[8,1024]{1,0:T(8,128)S(1)} %copy-done.6), kind=kOutput, calls=%fused_computation.1 | convolution fusion | flops 7523008512 | bytes 16809984 | tf_op jit(solution)/shard_map/dot_general | solution.py:20
  544.8 64.2 %all-gather.5.cloned.1.call-done = bf16[1024,3584]{1,0:T(8,128)(2,1)} async-done(((bf16[128,3584]{1,0:T(8,128)(2,1)}), bf16[1024,3584]{1,0:T(8,128)(2,1)}) %all-gather.5.cloned.1.call-update) | async-done | bytes 7340048 | tf_op jit(solution)/shard_map/all_gather | solution.py:80
  609.0 12.4 %bitcast_reduce_fusion = bf16[8,1024]{1,0:T(8,128)(2,1)S(1)} fusion(bf16[128,8,1024]{2,0,1:T(8,128)(2,1)} %copy-done.1, bf16[1024,3584]{1,0:T(8,128)(2,1)} %all-gather.5.cloned.1.call-done, bf16[3584,1024]{1,0:T(8,128)(2,1)} %param.27), kind=kOutput, calls=%fused_computation.8 | convolution fusion | flops 7519330304 | bytes 16793600 | tf_op jit(solution)/shard_map/dot_general | solution.py:101
  621.4 11.4 %all-reduce = (bf16[8,1024]{1,0:T(8,128)(2,1)S(1)}, bf16[8,1024]{1,0:T(8,128)(2,1)S(1)}) all-reduce(bf16[8,1024]{1,0:T(8,128)(2,1)S(1)} %get-tuple-element.22, bf16[8,1024]{1,0:T(8,128)(2,1)S(1)} %bitcast_reduce_fusion), channel_id=1, replica_groups=mesh['member'=8,'tensor'=4] {'tensor'}, use_global_device_ids=true, to_apply=%region_3.0 | all-reduce | flops 16384 | bytes 65536 | tf_op jit(solution)/shard_map/psum | solution.py:115
  634.1 12.8 %convolution_convert_fusion = bf16[3584,1024]{1,0:T(8,128)(2,1)} fusion(bf16[1024,3584]{1,0:T(8,128)(2,1)} %all-gather.5.cloned.1.call-done, bf16[1024,1024]{1,0:T(8,128)(2,1)} %copy-done.5), kind=kOutput, calls=%fused_computation.2 | convolution fusion | flops 7519862784 | bytes 16777216 | tf_op jit(solution)/shard_map/dot_general | solution.py:20
  650.4 13.0 %convolution_convert_fusion.1 = bf16[1024,3584]{1,0:T(8,128)(2,1)} fusion(bf16[1024,1024]{1,0:T(8,128)(2,1)S(1)} %copy-done.4, bf16[1024,3584]{1,0:T(8,128)(2,1)} %all-gather.3.cloned.1.call-done), kind=kOutput, calls=%fused_computation.3 | convolution fusion | flops 7519862784 | bytes 16777216 | tf_op jit(solution)/shard_map/dot_general | solution.py:20
  (75 shorter events, 42.7 us)
Async XLA Ops:
  7.2 201.4 %reduce-scatter.3.cloned.1.call-start = ((), (), s32[]{:S(2)}) async-start(), calls=%async_computation.5 | async-start | bytes 8257536 | tf_op jit(solution)/shard_map/reduce_scatter | solution.py:56
  7.2 57.4 %copy-start.7 = (f32[8,1024]{1,0:T(8,128)S(1)}, f32[8,1024]{1,0:T(8,128)}, u32[]{:S(2)}) copy-start(f32[8,1024]{1,0:T(8,128)} %param.18) | copy-start | bytes 98308
  9.0 57.6 %copy-start.12 = (bf16[3584,1024]{1,0:T(8,128)(2,1)S(1)}, bf16[3584,1024]{1,0:T(8,128)(2,1)}, u32[]{:S(2)}) copy-start(bf16[3584,1024]{1,0:T(8,128)(2,1)} %param.27) | copy-start | bytes 22020100
  64.6 11.8 %copy-start.1 = (bf16[128,8,1024]{2,0,1:T(8,128)(2,1)}, bf16[128,8,1024]{2,0,1:T(8,128)(2,1)S(1)}, u32[]{:S(2)}) copy-start(bf16[128,8,1024]{2,0,1:T(8,128)(2,1)S(1)} %all_to_all.44) | copy-start | bytes 6291460
  65.2 1.4 copy-start.5
  76.5 0.9 copy-start.11
  76.5 0.9 copy-start.13
  76.5 132.1 %copy-start.3 = (bf16[128,3584]{1,0:T(8,128)(2,1)S(1)}, bf16[128,3584]{1,0:T(8,128)(2,1)}, u32[]{:S(2)}) copy-start(bf16[128,3584]{1,0:T(8,128)(2,1)} %param.23) | copy-start | bytes 2752516
  76.5 428.3 %all-gather.3.cloned.1.call-start = ((), (), s32[]{:S(2)}) async-start(), calls=%async_computation.6 | async-start | bytes 8257536 | tf_op jit(solution)/shard_map/all_gather | solution.py:81
  218.1 81.6 %all-to-all-start.2 = ((bf16[128,8,1024]{0,2,1:T(8,128)(2,1)}), bf16[128,8,1024]{0,2,1:T(8,128)(2,1)S(1)}, u32[]{:S(2)}, u32[]{:S(2)}) async-start(bf16[128,8,1024]{0,2,1:T(8,128)(2,1)} %bitcast.77), calls=%async_computation.4 | async-start | bytes 4194304 | tf_op jit(solution)/shard_map/all_to_all | solution.py:51
  221.8 387.2 %all-gather.5.cloned.1.call-start = ((), (), s32[]{:S(2)}) async-start(), calls=%async_computation.8 | async-start | bytes 8257536 | tf_op jit(solution)/shard_map/all_gather | solution.py:80
  222.5 424.4 %reduce-scatter.5.cloned.1.call-start = ((), (), s32[]{:S(2)}) async-start(), calls=%async_computation.7 | async-start | bytes 2621440 | tf_op jit(solution)/shard_map/reduce_scatter | solution.py:119
  226.0 87.9 %collective-permute-start = (bf16[128,3584]{1,0:T(8,128)(2,1)}, bf16[128,3584]{1,0:T(8,128)(2,1)S(1)}, u32[]{:S(2)}, u32[]{:S(2)}) collective-permute-start(bf16[128,3584]{1,0:T(8,128)(2,1)} %get-tuple-element.20), channel_id=1, source_target_pairs={{0,4},{4,8},{8,12},{12,16},{16,20},{20,24},{24,28},{28,0},{1,5},{5... | collective-permute-start | bytes 2752520 | tf_op jit(solution)/shard_map/ppermute | solution.py:86
  302.0 5.4 copy-start.6
  314.0 61.6 %collective-permute-start.1 = (bf16[128,3584]{1,0:T(8,128)(2,1)S(1)}, bf16[128,3584]{1,0:T(8,128)(2,1)S(1)}, u32[]{:S(2)}, u32[]{:S(2)}) collective-permute-start(bf16[128,3584]{1,0:T(8,128)(2,1)S(1)} %collective-permute-done), channel_id=1, source_target_pairs={{0,4},{4,8},{8,12},{12,16},{16,20},{20,24},{24,28},{28,0},{1,5},{5... | collective-permute-start | bytes 2752520 | tf_op jit(solution)/shard_map/ppermute | solution.py:86
  375.6 41.6 %collective-permute-start.2 = (bf16[128,3584]{1,0:T(8,128)(2,1)S(1)}, bf16[128,3584]{1,0:T(8,128)(2,1)S(1)}, u32[]{:S(2)}, u32[]{:S(2)}) collective-permute-start(bf16[128,3584]{1,0:T(8,128)(2,1)S(1)} %collective-permute-done.1), channel_id=1, source_target_pairs={{0,4},{4,8},{8,12},{12,16},{16,20},{20,24},{24,28},{28,0},{1,5},{5... | collective-permute-start | bytes 2752520 | tf_op jit(solution)/shard_map/ppermute | solution.py:86
  417.2 20.5 %collective-permute-start.3 = (bf16[128,3584]{1,0:T(8,128)(2,1)S(1)}, bf16[128,3584]{1,0:T(8,128)(2,1)S(1)}, u32[]{:S(2)}, u32[]{:S(2)}) collective-permute-start(bf16[128,3584]{1,0:T(8,128)(2,1)S(1)} %collective-permute-done.2), channel_id=1, source_target_pairs={{0,4},{4,8},{8,12},{12,16},{16,20},{20,24},{24,28},{28,0},{1,5},{5... | collective-permute-start | bytes 2752520 | tf_op jit(solution)/shard_map/ppermute | solution.py:86
  437.7 20.5 %collective-permute-start.4 = (bf16[128,3584]{1,0:T(8,128)(2,1)S(1)}, bf16[128,3584]{1,0:T(8,128)(2,1)S(1)}, u32[]{:S(2)}, u32[]{:S(2)}) collective-permute-start(bf16[128,3584]{1,0:T(8,128)(2,1)S(1)} %collective-permute-done.3), channel_id=1, source_target_pairs={{0,4},{4,8},{8,12},{12,16},{16,20},{20,24},{24,28},{28,0},{1,5},{5... | collective-permute-start | bytes 2752520 | tf_op jit(solution)/shard_map/ppermute | solution.py:86
  458.3 20.5 %collective-permute-start.5 = (bf16[128,3584]{1,0:T(8,128)(2,1)S(1)}, bf16[128,3584]{1,0:T(8,128)(2,1)S(1)}, u32[]{:S(2)}, u32[]{:S(2)}) collective-permute-start(bf16[128,3584]{1,0:T(8,128)(2,1)S(1)} %collective-permute-done.4), channel_id=1, source_target_pairs={{0,4},{4,8},{8,12},{12,16},{16,20},{20,24},{24,28},{28,0},{1,5},{5... | collective-permute-start | bytes 2752520 | tf_op jit(solution)/shard_map/ppermute | solution.py:86
  478.8 18.0 %collective-permute-start.6 = (bf16[128,3584]{1,0:T(8,128)(2,1)S(1)}, bf16[128,3584]{1,0:T(8,128)(2,1)S(1)}, u32[]{:S(2)}, u32[]{:S(2)}) collective-permute-start(bf16[128,3584]{1,0:T(8,128)(2,1)S(1)} %collective-permute-done.5), channel_id=1, source_target_pairs={{0,4},{4,8},{8,12},{12,16},{16,20},{20,24},{24,28},{28,0},{1,5},{5... | collective-permute-start | bytes 2752520 | tf_op jit(solution)/shard_map/ppermute | solution.py:86
  504.9 14.2 %copy-start = (f32[8,128,1024]{2,1,0:T(8,128)S(1)}, f32[8,128,1024]{2,1,0:T(8,128)}, u32[]{:S(2)}) copy-start(f32[8,128,1024]{2,1,0:T(8,128)} %copy.27) | copy-start | bytes 12582916
  504.9 14.2 %copy-start.2 = (bf16[8,128,3584]{2,1,0:T(8,128)(2,1)S(1)}, bf16[8,128,3584]{2,1,0:T(8,128)(2,1)}, u32[]{:S(2)}) copy-start(bf16[8,128,3584]{2,1,0:T(8,128)(2,1)} %gather_fusion) | copy-start | bytes 22020100
  634.1 16.3 %copy-start.4 = (bf16[1024,1024]{1,0:T(8,128)(2,1)S(1)}, bf16[1024,1024]{1,0:T(8,128)(2,1)}, u32[]{:S(2)}) copy-start(bf16[1024,1024]{1,0:T(8,128)(2,1)} %fusion.2) | copy-start | bytes 6291460
  646.9 18.0 %all-to-all-start.1 = ((bf16[8,32,1024]{2,1,0:T(8,128)(2,1)}), bf16[8,32,1024]{2,1,0:T(8,128)(2,1)S(1)}, u32[]{:S(2)}, u32[]{:S(2)}) async-start(bf16[8,32,1024]{2,1,0:T(8,128)(2,1)} %reduce-scatter.5.cloned.1.call-done), calls=%async_computation.3 | async-start | bytes 1048576 | tf_op jit(solution)/shard_map/all_to_all | solution.py:122
  (3 other events, 2.3 us)
Sparse Core Ops, SparseCore 0:
  76.6 131.8 reduce-scatter.2
  214.2 183.3 all-gather.2
  399.8 209.1 all-gather.4
  611.4 29.5 reduce-scatter.4
